TPU v7x, 512 devices: a whole 4x4x16 slice. The times are simulated.
512 devices in a mesh: tr: 64 (over x, z), ct: 8 (over y, core).
Axes of the slice: x: 4, y: 4, z: 16, core: 2. Of those that a mesh axis runs over, the one named last changes fastest.
Arguments:
- amplitudes: bfloat16 [8, 4096, 2, 4096], P(None, 'tr', None, 'ct'), may hold values from -6 to 6
- cycle_integrals: bfloat16 [2, 4096, 1, 4096], P(None, 'ct', None, 'tr'), may hold values from -0.0625 to 0.0625
- pair_live: int32 [8, 64], replicated, may hold values 0 or 1
Outputs:
- permuted: bfloat16 [8, 4096, 1, 4096], P('ct', 'tr')
All inputs are finite; a program needn't handle non-finite values.
Results may differ from a plain program's by a relative error of at most 0.017.
Values may be sent and summed in bfloat16 or wider, within the bound.
A program may use at most 64 MiB of HBM per device.

v0:
```python
import jax
import jax.numpy as jnp
from jax import lax
from jax.sharding import PartitionSpec as P


def per_device(amplitudes, cycle_integrals, pair_live):
    tile_size = amplitudes.shape[1]
    block_cols = amplitudes.shape[3]
    occ_k = amplitudes.shape[2]
    row_index = lax.axis_index("tr")
    col_index = lax.axis_index("ct")
    row_live = lax.dynamic_slice_in_dim(pair_live, row_index, 1, 1).astype(jnp.bfloat16)
    col_full = jnp.repeat(pair_live[:occ_k], tile_size, axis=1)
    col_live = lax.dynamic_slice_in_dim(col_full, col_index * block_cols, block_cols, 1).astype(
        jnp.bfloat16
    )
    masked = amplitudes * row_live[:, :, None, None] * col_live[None, None, :, :]
    partial_value = jnp.einsum(
        "iakc,kcjb->iajb",
        masked,
        lax.all_gather(cycle_integrals, "tr", axis=3, tiled=True),
        preferred_element_type=jnp.float32,
    )
    moved_parts = lax.all_to_all(
        partial_value.astype(jnp.bfloat16), "tr", split_axis=3, concat_axis=1, tiled=True
    )
    moved = lax.psum_scatter(
        moved_parts.astype(jnp.float32).astype(jnp.bfloat16), "ct", scatter_dimension=0, tiled=True
    )
    return jnp.transpose(moved, (0, 3, 2, 1))


def solution(mesh):
    return jax.shard_map(
        per_device,
        mesh=mesh,
        in_specs=(P(None, "tr", None, "ct"), P(None, "ct", None, "tr"), P()),
        out_specs=P("ct", "tr", None, None),
        check_vma=False,
    )
```

profile of v0, /device:TPU:1, one launch (start us, length us, event | category | flops | bytes accessed | tf_op | source)
XLA Modules:
  0.0 499.4 jit_solution(14204285625697679978)
XLA Ops:
  6.5 0.0 all-gather.2.cloned.1.call-start
  6.5 1.7 copy.7
  8.2 0.0 all-gather.2.cloned.1.call-update
  8.3 0.0 reduce-scatter.2.cloned.1.call-start
  8.3 0.7 slice.3
  9.0 0.9 fusion.8
  9.9 0.1 broadcast_in_dim.2
  9.9 0.1 reshape.10
  10.1 2.3 multiply_multiply_fusion
  12.4 152.3 %all-gather.2.cloned.1.call-done = bf16[2,512,1,4096]{1,0,2,3:T(2,128)(2,1)} async-done(((bf16[2,512,1,64]{1,0,2,3:T(2,128)(2,1)}), bf16[2,512,1,4096]{1,0,2,3:T(2,128)(2,1)}) %all-gather.2.cloned.1.call-update) | async-done | bytes 8388624 | tf_op jit(solution)/shard_map/all_gather | solution.py:22
  164.7 21.3 %copy.8 = bf16[2,512,1,4096]{3,1,0,2:T(8,128)(2,1)} copy(bf16[2,512,1,4096]{1,0,2,3:T(2,128)(2,1)} %all-gather.2.cloned.1.call-done) | data formatting | bytes 16777216 | tf_op jit(solution)/shard_map/all_gather | solution.py:22
  185.9 9.4 %fusion.4 = bf16[8,64,1,4096]{3,1,0,2:T(8,128)(2,1)} fusion(bf16[2,512,1,4096]{3,1,0,2:T(8,128)(2,1)} %copy.8, bf16[8,64,2,512]{3,2,1,0:T(2,128)(2,1)S(1)} %multiply_multiply_fusion), kind=kOutput, calls=%fused_computation.3 | convolution fusion | flops 4297064448 | bytes 13631488 | tf_op jit(solution)/shard_map/iakc,kcjb->iajb/dot_general | solution.py:19
  195.3 10.0 %copy.10 = bf16[8,64,1,4096]{1,0,2,3:T(8,128)(2,1)} copy(bf16[8,64,1,4096]{3,1,0,2:T(8,128)(2,1)} %fusion.4) | data formatting | bytes 8388608 | tf_op jit(solution)/shard_map/convert_element_type | solution.py:26
  205.3 14.3 %reshape.15 = bf16[64,2,16384]{2,1,0:T(2,128)(2,1)} reshape(bf16[4096,1,8,64]{3,2,1,0:T(8,128)(2,1)} %bitcast.25) | data formatting | bytes 8388608
  219.7 184.9 %all_to_all.18 = bf16[64,2,16384]{2,1,0:T(2,128)(2,1)} all-to-all(bf16[64,2,16384]{2,1,0:T(2,128)(2,1)} %reshape.15), channel_id=1, replica_groups=mesh['tr'=64,'ct'=8] {'tr'}, dimensions={0} | all-to-all | bytes 8388608 | tf_op jit(solution)/shard_map/all_to_all | solution.py:25
  404.5 14.6 %reshape.16 = bf16[4096,1,8,64]{3,2,1,0:T(8,128)(2,1)} reshape(bf16[64,2,16384]{2,1,0:T(2,128)(2,1)} %all_to_all.18) | data formatting | bytes 8388608
  419.1 12.0 %copy.11 = bf16[8,64,64,1,64]{2,1,4,0,3:T(8,128)(2,1)} copy(bf16[8,64,64,1,64]{2,0,4,1,3:T(8,128)(2,1)} %bitcast.26) | data formatting | bytes 8388608 | tf_op jit(solution)/shard_map/all_to_all | solution.py:25
  431.1 12.1 %all_to_all.16 = bf16[8,4096,1,64]{1,3,2,0:T(8,128)(2,1)} reshape(bf16[8,64,64,1,64]{2,1,4,0,3:T(8,128)(2,1)} %copy.11) | data formatting | bytes 8388608 | tf_op jit(solution)/shard_map/all_to_all | solution.py:25
  443.2 0.0 reduce-scatter.2.cloned.1.call-update
  443.2 49.3 %reduce-scatter.2.cloned.1.call-done = bf16[1,4096,1,64]{1,3,2,0:T(8,128)(2,1)} async-done(((bf16[8,4096,1,64]{1,3,2,0:T(8,128)(2,1)}), bf16[1,4096,1,64]{1,3,2,0:T(8,128)(2,1)}) %reduce-scatter.2.cloned.1.call-update) | async-done | bytes 524304 | tf_op jit(solution)/shard_map/reduce_scatter | solution.py:28
  (1 shorter events, 0.0 us)
Async XLA Ops:
  6.5 158.1 %all-gather.2.cloned.1.call-start = ((), (), s32[]{:S(2)}) async-start(), calls=%async_computation.2 | async-start | bytes 8519680 | tf_op jit(solution)/shard_map/all_gather | solution.py:22
  8.3 484.3 %reduce-scatter.2.cloned.1.call-start = ((), (), s32[]{:S(2)}) async-start(), calls=%async_computation.3 | async-start | bytes 4718592 | tf_op jit(solution)/shard_map/reduce_scatter | solution.py:28
Sparse Core Ops, SparseCore 0:
  10.3 154.3 all-gather.1
  443.3 49.1 reduce-scatter.1
where the time goes:
time: 503 us; the launch traced here: 499 us
  waiting for transfers between devices  202 us (40%)
  blocking collectives  185 us (37%)
  local copies, waits for them, and re-layouts  86.8 us (17%)
  between operations  13.4 us (3%)
  matrix products  9.39 us (2%)
    all_to_all x1, blocking collectives, per_device(): lax.all_to_all(partial_value.astype(jnp.bfloat16), 'tr', split_axis=3, co...  185 us
    all_gather x1, waiting for transfers between devices, per_device(): lax.all_gather(cycle_integrals, 'tr', axis=3, tiled=True)  152 us
    reduce_scatter x1, waiting for transfers between devices, per_device(): lax.psum_scatter(moved_parts.astype(jnp.float32).astype(jnp.bfloat16), 'c...  49.3 us
    unnamed x3, local copies, waits for them, and re-layouts  30.6 us
    all_to_all x2, local copies, waits for them, and re-layouts, per_device(): lax.all_to_all(partial_value.astype(jnp.bfloat16), 'tr', split_axis=3, co...  24 us
    all_gather x1, local copies, waits for them, and re-layouts, per_device(): lax.all_gather(cycle_integrals, 'tr', axis=3, tiled=True)  21.3 us
  transfers between devices with their start and end apart: 2, of which 2 were waited for; matrix products, arithmetic and copies ran while one was open for 1% of the time, Pallas kernels for 0%

commit v1 on v0

v1 whole, which is shorter than its diff:
```python
import functools

import jax
import jax.numpy as jnp
from jax import lax
from jax.experimental import pallas as pl
from jax.experimental.pallas import tpu as pltpu
from jax.sharding import PartitionSpec as P

MESH = pl.DeviceIdType.MESH
F32 = jnp.float32
BF16 = jnp.bfloat16
NZ = 16


def dot_nt(lhs, rhs):
    return lax.dot_general(lhs, rhs, (((1,), (1,)), ((), ())), preferred_element_type=F32)


def kernel(
    a_ref, w_ref, out_ref,
    abuf, wbuf, kept, csend, crecv, y1send, y1recv, y2send, y2recv, psend, pieces,
    s_a, s_af, r_a, s_w, r_w, s_c, r_c, s_y1, r_y1, s_y2, r_y2, s_p, r_p,
):
    t_index = lax.axis_index("tr")
    c_index = lax.axis_index("ct")
    x, z = t_index // NZ, t_index % NZ
    y, q = c_index // 2, c_index % 2
    yn1 = y + 1 - 2 * (y % 2)
    yn3 = 3 - y
    yop = (y + 2) % 4

    def dev(xx, yy, zz, qq):
        return (xx * NZ + zz, yy * 2 + qq)

    xp, xm = dev((x + 1) % 4, y, z, q), dev((x + 3) % 4, y, z, q)
    zp, zm = dev(x, y, (z + 1) % NZ, q), dev(x, y, (z + NZ - 1) % NZ, q)
    mate = dev(x, y, z, 1 - q)

    def rcopy(src, dst, ssem, rsem, to):
        return pltpu.make_async_remote_copy(
            src_ref=src, dst_ref=dst, send_sem=ssem, recv_sem=rsem, device_id=to, device_id_type=MESH
        )

    barrier = pltpu.get_barrier_semaphore()

    def greet(n, carry):
        zz, qq = n // 2, n % 2

        @pl.when(n != z * 2 + q)
        def _():
            pl.semaphore_signal(barrier, inc=1, device_id=dev(x, y, zz, qq), device_id_type=MESH)

        return carry

    for other in (xp, xm, dev(x, yn1, z, q), dev(x, yn3, z, q)):
        pl.semaphore_signal(barrier, inc=1, device_id=other, device_id_type=MESH)
    lax.fori_loop(0, 2 * NZ, greet, 0)
    pl.semaphore_wait(barrier, 2 * NZ - 1 + 4)

    def a_own(side, chunk):
        rows = pl.ds(chunk * 128, 128)
        return rcopy(a_ref.at[:, rows], abuf.at[side, :, rows], s_a.at[side, chunk], r_a.at[side, chunk],
                     (xp, xm)[side])

    def a_fwd(side, chunk):
        rows = pl.ds(chunk * 128, 128)
        return rcopy(abuf.at[side, :, rows], abuf.at[2, :, rows], s_af.at[chunk], r_a.at[2, chunk],
                     (xp, xm)[side])

    def w_hop(way, step, half):
        src = w_ref.at[half] if step == 1 else wbuf.at[way, step - 2, half]
        dst = wbuf.at[1, 7, half] if step == 8 else wbuf.at[way, step - 1, half]
        return rcopy(src, dst, s_w.at[way, step - 1, half], r_w.at[way, step - 1, half], (zm, zp)[way])

    for half in range(2):
        for way in range(2):
            w_hop(way, 1, half).start()
    for order in range(4):
        a_own(0, order).start()
        a_own(1, (order + 2) % 4).start()
    wbuf[0, 7] = w_ref[...]

    def compute(t, h, blocks):
        def pair(p, carry):
            total = jnp.zeros((512, 256), F32)
            for k in range(2):
                mine = wbuf[q, pl.ds(h * 4, 4), k].reshape(256, 512)
                theirs = wbuf[1 - q, pl.ds(h * 4, 4), k].reshape(256, 512)
                rows = jnp.concatenate([mine, theirs], axis=0)
                total = total + dot_nt(rows, blocks[k, pl.ds(pl.multiple_of(p * 256, 256), 256)])
            for n in range(2):
                cols = total[:, n * 128:(n + 1) * 128]
                kept[t, p * 2 + n] = cols[:256]
                csend[t, p * 2 + n] = cols[256:].astype(BF16)
            return carry

        lax.fori_loop(0, 2, pair, 0)
        c_copy(t).start()

    def c_copy(t):
        return rcopy(csend.at[t], crecv.at[t], s_c.at[t], r_c.at[t], mate)

    def partners(h):
        return (1 - h) * yn1 + h * yn3, (1 - h) * yn3 + h * yn1

    def y1_copy(t, h):
        return rcopy(y1send.at[t], y1recv.at[t], s_y1.at[t], r_y1.at[t], dev(x, partners(h)[0], z, q))

    def y2_copy(t, h):
        return rcopy(y2send.at[t], y2recv.at[t], s_y2.at[t], r_y2.at[t], dev(x, partners(h)[1], z, q))

    def core_sum(t, h):
        c_copy(t).wait_recv()
        near, far = partners(h)
        y1send[t, 0] = (kept[t, near] + crecv[t, near].astype(F32)).astype(BF16)
        y1send[t, 1] = (kept[t, yop] + crecv[t, yop].astype(F32)).astype(BF16)
        y1_copy(t, h).start()
        kept[t, y] = kept[t, y] + crecv[t, y].astype(F32)
        kept[t, far] = kept[t, far] + crecv[t, far].astype(F32)

    def y_sum1(t, h):
        y1_copy(t, h).wait_recv()
        far = partners(h)[1]
        y2send[t] = (kept[t, far] + y1recv[t, 1].astype(F32)).astype(BF16)
        y2_copy(t, h).start()
        kept[t, y] = kept[t, y] + y1recv[t, 0].astype(F32)

    def target(h, s):
        slot = h * 4 + s
        off = (1 - q) * ((slot + 1) % 8) + q * (15 - slot)
        return (z + off) % NZ, slot

    def p_copy(t, h, stage, s, i):
        there = target(h, s)[0]
        return rcopy(psend.at[t, s, i], pieces.at[stage, z], s_p.at[t, s, i], r_p.at[stage, z],
                     dev(x, y, there, i))

    low = lax.broadcasted_iota(jnp.int32, (32, 128), 1) < 64

    def y_sum2(t, h, stage):
        y2_copy(t, h).wait_recv()
        for s in range(4):
            full = kept[t, y, s * 64:(s + 1) * 64] + y2recv[t, s * 64:(s + 1) * 64].astype(F32)
            top, bottom = full[:32], full[32:]
            psend[t, s, 0] = jnp.where(low, top, pltpu.roll(bottom, 64, 1)).astype(BF16)
            psend[t, s, 1] = jnp.where(low, pltpu.roll(top, 64, 1), bottom).astype(BF16)
        for s in range(4):
            own = (target(h, s)[1] == 7) & (q == 0)

            @pl.when(own)
            def _():
                pieces[stage, z] = psend[t, s, 0]

            @pl.when(jnp.logical_not(own))
            def _():
                p_copy(t, h, stage, s, 0).start()

            p_copy(t, h, stage, s, 1).start()

    def ring(step):
        for half in range(2):
            for way in range(2):
                w_hop(way, step - 1, half).wait_recv()
                if step < 8 or half == 1 - way:
                    w_hop(way, step, half).start()

    ring(2)
    ring(3)
    a_own(0, 0).wait_recv()
    a_fwd(0, 0).start()
    a_own(1, 2).wait_recv()
    a_fwd(1, 2).start()
    ring(4)
    ring(5)
    compute(0, 0, a_ref)
    a_own(0, 1).wait_recv()
    a_fwd(0, 1).start()
    a_own(1, 3).wait_recv()
    a_fwd(1, 3).start()
    ring(6)
    core_sum(0, 0)
    ring(7)
    y_sum1(0, 0)
    ring(8)
    y_sum2(0, 0, 0)
    w_hop(0, 8, 1).wait_recv()
    w_hop(1, 8, 0).wait_recv()
    compute(1, 1, a_ref)
    for chunk in range(2):
        a_own(0, chunk + 2).wait_recv()
        a_own(1, chunk).wait_recv()

    def step(t, carry):
        h, hh = t % 2, (t + 1) % 2

        @pl.when(t == 6)
        def _():
            for chunk in range(4):
                a_fwd(chunk // 2, chunk).wait_recv()

        @pl.when(t < 8)
        def _():
            compute(t, h, abuf.at[t // 2 - 1])

        @pl.when(t < 9)
        def _():
            core_sum(t - 1, hh)

        @pl.when((t > 2) & (t < 10))
        def _():
            y_sum1(t - 2, h)

        @pl.when(t > 3)
        def _():
            y_sum2(t - 3, hh, (t - 3) // 2)

        return carry

    lax.fori_loop(2, 11, step, 0)

    for stage in range(4):
        xs = (x + (0, 3, 1, 2)[stage]) % 4

        def arrive(n, carry):
            @pl.when((n != z) | (q != 0))
            def _():
                rcopy(psend.at[0, 0, 0], pieces.at[stage, n], s_p.at[0, 0, 0], r_p.at[stage, n],
                      mate).wait_recv()

            return carry

        lax.fori_loop(0, NZ, arrive, 0)
        for m in range(NZ // 2):
            even, odd = pieces[stage, 2 * m].astype(F32), pieces[stage, 2 * m + 1].astype(F32)
            cols = pl.ds(pl.multiple_of(xs * 1024 + m * 128, 128), 128)
            out_ref[0:32, cols] = jnp.where(low, even, pltpu.roll(odd, 64, 1)).astype(BF16)
            out_ref[32:64, cols] = jnp.where(low, pltpu.roll(even, 64, 1), odd).astype(BF16)

    for way in range(2):
        for n in range(1, 9):
            for half in range(2):
                if n < 8 or half == 1 - way:
                    w_hop(way, n, half).wait_send()
        for chunk in range(4):
            a_own(way, chunk).wait_send()
    for chunk in range(4):
        a_fwd(chunk // 2, chunk).wait_send()

    def drain(t, carry):
        h = t % 2
        c_copy(t).wait_send()
        y1_copy(t, h).wait_send()
        y2_copy(t, h).wait_send()
        for s in range(4):
            own = (target(h, s)[1] == 7) & (q == 0)

            @pl.when(jnp.logical_not(own))
            def _():
                p_copy(t, h, t // 2, s, 0).wait_send()

            p_copy(t, h, t // 2, s, 1).wait_send()
        return carry

    lax.fori_loop(0, 8, drain, 0)


def fused(blocks, tiles):
    dma = pltpu.SemaphoreType.DMA
    return pl.pallas_call(
        kernel,
        out_shape=jax.ShapeDtypeStruct((64, 4096), BF16),
        in_specs=[pl.BlockSpec(memory_space=pltpu.VMEM)] * 2,
        out_specs=pl.BlockSpec(memory_space=pltpu.VMEM),
        scratch_shapes=[
            pltpu.VMEM((3, 2, 512, 512), BF16),
            pltpu.VMEM((2, 8, 2, 64, 512), BF16),
            pltpu.VMEM((8, 4, 256, 128), F32),
            pltpu.VMEM((8, 4, 256, 128), BF16),
            pltpu.VMEM((8, 4, 256, 128), BF16),
            pltpu.VMEM((8, 2, 256, 128), BF16),
            pltpu.VMEM((8, 2, 256, 128), BF16),
            pltpu.VMEM((8, 256, 128), BF16),
            pltpu.VMEM((8, 256, 128), BF16),
            pltpu.VMEM((8, 4, 2, 32, 128), BF16),
            pltpu.VMEM((4, NZ, 32, 128), BF16),
            dma((2, 4)), dma((4,)), dma((3, 4)),
            dma((2, 8, 2)), dma((2, 8, 2)),
            dma((8,)), dma((8,)), dma((8,)), dma((8,)), dma((8,)), dma((8,)),
            dma((8, 4, 2)), dma((4, NZ)),
        ],
        compiler_params=pltpu.CompilerParams(
            collective_id=0, has_side_effects=True, vmem_limit_bytes=48 * 1024 * 1024
        ),
        name="cycle_fused",
    )(blocks, tiles)


def per_device(amplitudes, cycle_integrals, pair_live):
    row_index = lax.axis_index("tr")
    col_index = lax.axis_index("ct")
    row_live = lax.dynamic_slice_in_dim(pair_live, row_index, 1, 1).astype(BF16)
    col_full = jnp.repeat(pair_live[:2], 64, axis=1)
    col_live = lax.dynamic_slice_in_dim(col_full, col_index * 512, 512, 1).astype(BF16)
    masked = amplitudes * row_live[:, :, None, None] * col_live[None, None, :, :]
    blocks = masked.transpose(2, 0, 1, 3).reshape(2, 512, 512)
    tiles = cycle_integrals[:, :, 0, :].transpose(0, 2, 1)
    return fused(blocks, tiles).reshape(1, 64, 1, 4096)


def solution(mesh):
    return jax.shard_map(
        per_device,
        mesh=mesh,
        in_specs=(P(None, "tr", None, "ct"), P(None, "ct", None, "tr"), P()),
        out_specs=P("ct", "tr", None, None),
        check_vma=False,
    )
```

time: 503 us -> 97.2 us (0.19)
  waiting for transfers between devices: 202 us -> 0 us
  blocking collectives: 185 us -> 0 us
  Pallas kernels: 0 us -> 91.2 us
  local copies, waits for them, and re-layouts: 86.8 us -> 3.22 us
  between operations: 13.4 us -> 0.05 us
  matrix products: 9.39 us -> 0 us
    all_to_all x1 -> x0, blocking collectives: 185 us -> none  [per_device(): lax.all_to_all(partial_value.astype(jnp.bfloat16), 'tr', split_axis=3, co...]
    all_gather x1 -> x0, waiting for transfers between devices: 152 us -> none  [per_device(): lax.all_gather(cycle_integrals, 'tr', axis=3, tiled=True)]
    pallas_call x0 -> x1, Pallas kernels: none -> 91.2 us  [fused(): pl.pallas_call(kernel, out_shape=jax.ShapeDtypeStruct((64, 4096), BF16),...]
    reduce_scatter x1 -> x0, waiting for transfers between devices: 49.3 us -> none  [per_device(): lax.psum_scatter(moved_parts.astype(jnp.float32).astype(jnp.bfloat16), 'c...]
    unnamed x3 -> x5, local copies, waits for them, and re-layouts: 30.6 us -> 2.17 us
    all_to_all x2 -> x0, local copies, waits for them, and re-layouts: 24 us -> none  [per_device(): lax.all_to_all(partial_value.astype(jnp.bfloat16), 'tr', split_axis=3, co...]
    all_gather x1 -> x0, local copies, waits for them, and re-layouts: 21.3 us -> none  [per_device(): lax.all_gather(cycle_integrals, 'tr', axis=3, tiled=True)]
    convert_element_type x1 -> x0, local copies, waits for them, and re-layouts: 10 us -> none  [per_device(): partial_value.astype(jnp.bfloat16)]
  transfers between devices with their start and end apart: 2 -> 0, of which waited for: 2 -> 0; matrix products, arithmetic and copies ran while one was open for 1% -> 0% of each run, Pallas kernels for 0% -> 0%
where the time goes in v1:
time: 97.2 us; the launch traced here: 97 us
  Pallas kernels  91.2 us (94%)
  local copies, waits for them, and re-layouts  3.22 us (3%)
  other arithmetic  2.5 us (3%)
    pallas_call x1, Pallas kernels, fused(): pl.pallas_call(kernel, out_shape=jax.ShapeDtypeStruct((64, 4096), BF16),...  91.2 us
    transpose x1, other arithmetic, per_device(): blocks = masked.transpose(2, 0, 1, 3).reshape(2, 512, 512)  2.3 us
    unnamed x5, local copies, waits for them, and re-layouts  2.17 us

profile of v1, /device:TPU:1, one launch (start us, length us, event | category | flops | bytes accessed | tf_op | source)
XLA Modules:
  0.0 97.0 jit_solution(9143682549586300696)
XLA Ops:
  0.0 0.0 copy-start.1
  0.0 0.7 copy-done.1
  0.7 0.2 fusion
  0.9 0.0 slice-start
  0.9 0.7 slice-done
  1.6 0.1 broadcast_in_dim.2
  1.6 0.1 reshape.11
  1.8 2.3 %multiply_bitcast_fusion = bf16[2,8,64,512]{3,0,2,1:T(2,128)(2,1)S(1)} fusion(bf16[8,64,2,512]{3,2,1,0:T(2,128)(2,1)} %param.3, bf16[8]{0:T(256)(128)(2,1)S(1)} %fusion, bf16[2,512]{1,0:T(2,128)(2,1)S(1)} %dynamic-slice_convert_fusion), kind=kLoop, calls=%fused_computation | loop fusion | flops 1048576 | bytes 2099216 | tf_op jit(solution)/shard_map/transpose | solution.py:306
  4.1 0.0 copy-start
  4.1 0.2 copy.4
  4.3 0.7 copy-done
  5.0 91.2 %cycle_fused.1 = bf16[64,4096]{1,0:T(8,128)(2,1)S(1)} custom-call(bf16[2,512,512]{2,1,0:T(8,128)(2,1)S(1)} %bitcast.7, bf16[2,64,512]{2,1,0:T(8,128)(2,1)S(1)} %bitcast.9), custom_call_target="tpu_custom_call" | custom-call | tf_op jit(solution)/shard_map/cycle_fused/pallas_call | solution.py:270
  96.2 0.8 copy.6
  (1 shorter events, 0.0 us)
Async XLA Ops:
  0.0 0.7 copy-start.1
  0.9 0.7 slice-start
  4.1 0.9 copy-start

commit v2 on v0

v2 whole, which is shorter than its diff:
```python
import functools

import jax
import jax.numpy as jnp
from jax import lax
from jax.experimental import pallas as pl
from jax.experimental.pallas import tpu as pltpu
from jax.sharding import PartitionSpec as P

MESH = pl.DeviceIdType.MESH
F32 = jnp.float32
BF16 = jnp.bfloat16
NZ = 16


def dot_nt(lhs, rhs):
    return lax.dot_general(lhs, rhs, (((1,), (1,)), ((), ())), preferred_element_type=F32)


def kernel(
    a_hbm, w_hbm, live_hbm, out_ref,
    raw, live, aown, abuf, wbuf, kept, csend, crecv, y1send, y1recv, y2send, y2recv, psend, pieces,
    s_in, s_a, s_af, r_a, s_w, r_w, s_c, r_c, s_y1, r_y1, s_y2, r_y2, s_p, r_p,
):
    t_index = lax.axis_index("tr")
    c_index = lax.axis_index("ct")
    x, z = t_index // NZ, t_index % NZ
    y, q = c_index // 2, c_index % 2
    yn1 = y + 1 - 2 * (y % 2)
    yn3 = 3 - y
    yop = (y + 2) % 4

    def dev(xx, yy, zz, qq):
        return (xx * NZ + zz, yy * 2 + qq)

    xp, xm = dev((x + 1) % 4, y, z, q), dev((x + 3) % 4, y, z, q)
    zp, zm = dev(x, y, (z + 1) % NZ, q), dev(x, y, (z + NZ - 1) % NZ, q)
    mate = dev(x, y, z, 1 - q)
    ynear, yfar = dev(x, yn1, z, q), dev(x, yn3, z, q)

    def rcopy(src, dst, ssem, rsem, to):
        return pltpu.make_async_remote_copy(
            src_ref=src, dst_ref=dst, send_sem=ssem, recv_sem=rsem, device_id=to, device_id_type=MESH
        )

    barrier = pltpu.get_barrier_semaphore()
    for other in (zp, zm, xp, xm, mate, ynear, yfar):
        pl.semaphore_signal(barrier, inc=1, device_id=other, device_id_type=MESH)

    live_in = pltpu.make_async_copy(live_hbm, live, s_in.at[0])
    w_in = pltpu.make_async_copy(w_hbm, wbuf.at[0, 7], s_in.at[1])
    a_in = [
        pltpu.make_async_copy(a_hbm.at[pl.ds(2 * n, 2)], raw.at[pl.ds(2 * n, 2)], s_in.at[2 + n])
        for n in range(4)
    ]
    live_in.start()
    for n in (0, 2, 1, 3):
        a_in[n].start()
    w_in.start()

    def a_own(side, chunk):
        rows = pl.ds(chunk * 128, 128)
        return rcopy(aown.at[:, rows], abuf.at[side, :, rows], s_a.at[side, chunk], r_a.at[side, chunk],
                     (xp, xm)[side])

    def a_fwd(side, chunk):
        rows = pl.ds(chunk * 128, 128)
        return rcopy(abuf.at[side, :, rows], abuf.at[2, :, rows], s_af.at[chunk], r_a.at[2, chunk],
                     (xp, xm)[side])

    def w_hop(way, step, part):
        k, rows = part // 2, pl.ds((part % 2) * 32, 32)
        src = wbuf.at[0, 7, k, rows] if step == 1 else wbuf.at[way, step - 2, k, rows]
        dst = wbuf.at[1, 7, k, rows] if step == 8 else wbuf.at[way, step - 1, k, rows]
        return rcopy(src, dst, s_w.at[way, step - 1, part], r_w.at[way, step - 1, part], (zm, zp)[way])

    def carried(way, step, part):
        return step < 8 or part // 2 == 1 - way

    live_in.wait()
    block = lax.broadcasted_iota(jnp.int32, (1, 512), 1) // 64
    col = []
    for k in range(2):
        line = jnp.zeros((1, 512), F32)
        for n in range(8):
            line = jnp.where(block == n, live[k, c_index * 8 + n].astype(F32), line)
        col.append(line)

    def mask_chunk(n):
        a_in[n].wait()
        for i in (2 * n, 2 * n + 1):
            both = jnp.transpose(raw[i], (1, 0, 2))
            row = live[i, t_index].astype(F32)
            for k in range(2):
                aown[k, i * 64:(i + 1) * 64] = both[k] * (col[k] * row).astype(BF16)

    mask_chunk(0)
    mask_chunk(2)
    w_in.wait()
    pl.semaphore_wait(barrier, 7)
    for part in range(4):
        for way in range(2):
            w_hop(way, 1, part).start()
    a_own(0, 0).start()
    a_own(1, 2).start()
    mask_chunk(1)
    mask_chunk(3)
    for order in range(1, 4):
        a_own(0, order).start()
        a_own(1, (order + 2) % 4).start()

    def c_copy(t):
        return rcopy(csend.at[t], crecv.at[t], s_c.at[t], r_c.at[t], mate)

    def y1_copy(t, n):
        return rcopy(y1send.at[t, n], y1recv.at[t, n], s_y1.at[t, n], r_y1.at[t, n],
                     (ynear, yfar)[t % 2])

    def y2_copy(t):
        return rcopy(y2send.at[t], y2recv.at[t], s_y2.at[t], r_y2.at[t], (yfar, ynear)[t % 2])

    def compute(t):
        h = t % 2
        blocks = aown if t < 2 else abuf.at[t // 2 - 1]

        def pair(p, carry):
            total = jnp.zeros((512, 256), F32)
            for k in range(2):
                mine = wbuf[q, h * 4:h * 4 + 4, k].reshape(256, 512)
                theirs = wbuf[1 - q, h * 4:h * 4 + 4, k].reshape(256, 512)
                rows = jnp.concatenate([mine, theirs], axis=0)
                total = total + dot_nt(rows, blocks[k, pl.ds(pl.multiple_of(p * 256, 256), 256)])
            for n in range(2):
                cols = total[:, n * 128:(n + 1) * 128]
                kept[t, p * 2 + n] = cols[:256]
                csend[t, p * 2 + n] = cols[256:].astype(BF16)
            return carry

        lax.fori_loop(0, 2, pair, 0)
        c_copy(t).start()

    def core_sum(t):
        near, far = (yn1, yn3) if t % 2 == 0 else (yn3, yn1)
        c_copy(t).wait_recv()
        y1send[t, 1] = (kept[t, yop] + crecv[t, yop].astype(F32)).astype(BF16)
        y1_copy(t, 1).start()
        y1send[t, 0] = (kept[t, near] + crecv[t, near].astype(F32)).astype(BF16)
        y1_copy(t, 0).start()
        kept[t, far] = kept[t, far] + crecv[t, far].astype(F32)
        kept[t, y] = kept[t, y] + crecv[t, y].astype(F32)

    def y_sum1(t):
        far = (yn3, yn1)[t % 2]
        y1_copy(t, 1).wait_recv()
        y2send[t] = (kept[t, far] + y1recv[t, 1].astype(F32)).astype(BF16)
        y2_copy(t).start()

    def off(slot):
        return (1 - q) * ((slot + 1) % 8) + q * (15 - slot)

    def p_copy(t, s, i):
        return rcopy(psend.at[t, s, i], pieces.at[t // 2, z], s_p.at[t, s, i], r_p.at[t // 2, z],
                     dev(x, y, (z + off((t % 2) * 4 + s)) % NZ, i))

    low = lax.broadcasted_iota(jnp.int32, (32, 128), 1) < 64

    def y_sum2(t):
        y1_copy(t, 0).wait_recv()
        y2_copy(t).wait_recv()
        for s in range(4):
            rows = slice(s * 64, (s + 1) * 64)
            full = kept[t, y, rows] + y1recv[t, 0, rows].astype(F32) + y2recv[t, rows].astype(F32)
            top, bottom = full[:32], full[32:]
            psend[t, s, 0] = jnp.where(low, top, pltpu.roll(bottom, 64, 1)).astype(BF16)
            psend[t, s, 1] = jnp.where(low, pltpu.roll(top, 64, 1), bottom).astype(BF16)
        for s in range(4):
            p_copy(t, s, 1).start()
            if t % 2 == 1 and s == 3:
                @pl.when(q == 0)
                def _():
                    pieces[t // 2, z] = psend[t, s, 0]

                @pl.when(q != 0)
                def _():
                    p_copy(t, s, 0).start()
            else:
                p_copy(t, s, 0).start()

    def ring(step):
        for part in range(4):
            for way in range(2):
                w_hop(way, step - 1, part).wait_recv()
                if carried(way, step, part):
                    w_hop(way, step, part).start()

    def forward(first):
        for side in range(2):
            chunk = first + 2 * side
            a_own(side, chunk).wait_recv()
            a_fwd(side, chunk).start()

    ring(2)
    ring(3)
    forward(0)
    ring(4)
    ring(5)
    compute(0)
    forward(1)
    ring(6)
    core_sum(0)
    ring(7)
    y_sum1(0)
    ring(8)
    for part in range(2):
        w_hop(0, 8, part + 2).wait_recv()
        w_hop(1, 8, part).wait_recv()
    compute(1)
    a_own(0, 2).wait_recv()
    a_own(0, 3).wait_recv()
    compute(2)
    core_sum(1)
    y_sum2(0)
    compute(3)
    core_sum(2)
    a_own(1, 0).wait_recv()
    a_own(1, 1).wait_recv()
    compute(4)
    core_sum(3)
    compute(5)
    core_sum(4)
    y_sum1(1)
    core_sum(5)
    y_sum1(2)
    y_sum1(3)
    y_sum2(1)
    y_sum1(4)
    for chunk in range(4):
        a_fwd(chunk // 2, chunk).wait_recv()
    compute(6)
    y_sum1(5)
    y_sum2(2)
    compute(7)
    core_sum(6)
    y_sum2(3)
    core_sum(7)
    y_sum2(4)
    y_sum2(5)
    y_sum1(6)
    y_sum1(7)
    y_sum2(6)
    y_sum2(7)

    for stage in range(4):
        xs = (x + (0, 3, 1, 2)[stage]) % 4

        def arrive(n, carry):
            @pl.when((n != z) | (q != 0))
            def _():
                rcopy(psend.at[0, 0, 0], pieces.at[stage, n], s_p.at[0, 0, 0], r_p.at[stage, n],
                      mate).wait_recv()

            return carry

        lax.fori_loop(0, NZ, arrive, 0)
        for m in range(NZ // 2):
            even, odd = pieces[stage, 2 * m].astype(F32), pieces[stage, 2 * m + 1].astype(F32)
            cols = pl.ds(pl.multiple_of(xs * 1024 + m * 128, 128), 128)
            out_ref[0:32, cols] = jnp.where(low, even, pltpu.roll(odd, 64, 1)).astype(BF16)
            out_ref[32:64, cols] = jnp.where(low, pltpu.roll(even, 64, 1), odd).astype(BF16)

    for way in range(2):
        for n in range(1, 9):
            for part in range(4):
                if carried(way, n, part):
                    w_hop(way, n, part).wait_send()
        for chunk in range(4):
            a_own(way, chunk).wait_send()
    for chunk in range(4):
        a_fwd(chunk // 2, chunk).wait_send()
    for t in range(8):
        c_copy(t).wait_send()
        y1_copy(t, 0).wait_send()
        y1_copy(t, 1).wait_send()
        y2_copy(t).wait_send()
        for s in range(4):
            p_copy(t, s, 1).wait_send()
            if t % 2 == 1 and s == 3:
                @pl.when(q != 0)
                def _():
                    p_copy(t, s, 0).wait_send()
            else:
                p_copy(t, s, 0).wait_send()


def fused(amplitudes, tiles, pair_live):
    dma = pltpu.SemaphoreType.DMA
    return pl.pallas_call(
        kernel,
        out_shape=jax.ShapeDtypeStruct((64, 4096), BF16),
        in_specs=[pl.BlockSpec(memory_space=pl.ANY)] * 3,
        out_specs=pl.BlockSpec(memory_space=pltpu.VMEM),
        scratch_shapes=[
            pltpu.VMEM((8, 64, 2, 512), BF16),
            pltpu.SMEM((8, 64), jnp.int32),
            pltpu.VMEM((2, 512, 512), BF16),
            pltpu.VMEM((3, 2, 512, 512), BF16),
            pltpu.VMEM((2, 8, 2, 64, 512), BF16),
            pltpu.VMEM((8, 4, 256, 128), F32),
            pltpu.VMEM((8, 4, 256, 128), BF16),
            pltpu.VMEM((8, 4, 256, 128), BF16),
            pltpu.VMEM((8, 2, 256, 128), BF16),
            pltpu.VMEM((8, 2, 256, 128), BF16),
            pltpu.VMEM((8, 256, 128), BF16),
            pltpu.VMEM((8, 256, 128), BF16),
            pltpu.VMEM((8, 4, 2, 32, 128), BF16),
            pltpu.VMEM((4, NZ, 32, 128), BF16),
            dma((6,)), dma((2, 4)), dma((4,)), dma((3, 4)),
            dma((2, 8, 4)), dma((2, 8, 4)),
            dma((8,)), dma((8,)), dma((8, 2)), dma((8, 2)), dma((8,)), dma((8,)),
            dma((8, 4, 2)), dma((4, NZ)),
        ],
        compiler_params=pltpu.CompilerParams(
            collective_id=0, has_side_effects=True, vmem_limit_bytes=56 * 1024 * 1024
        ),
        name="cycle_fused",
    )(amplitudes, tiles, pair_live)


def per_device(amplitudes, cycle_integrals, pair_live):
    tiles = cycle_integrals[:, :, 0, :].transpose(0, 2, 1)
    return fused(amplitudes, tiles, pair_live).reshape(1, 64, 1, 4096)


def solution(mesh):
    return jax.shard_map(
        per_device,
        mesh=mesh,
        in_specs=(P(None, "tr", None, "ct"), P(None, "ct", None, "tr"), P()),
        out_specs=P("ct", "tr", None, None),
        check_vma=False,
    )
```

time: 503 us -> 85.9 us (0.17)
  waiting for transfers between devices: 202 us -> 0 us
  blocking collectives: 185 us -> 0 us
  local copies, waits for them, and re-layouts: 86.8 us -> 1.87 us
  Pallas kernels: 0 us -> 83.9 us
  between operations: 13.4 us -> 0.01 us
  matrix products: 9.39 us -> 0 us
    all_to_all x1 -> x0, blocking collectives: 185 us -> none  [per_device(): lax.all_to_all(partial_value.astype(jnp.bfloat16), 'tr', split_axis=3, co...]
    all_gather x1 -> x0, waiting for transfers between devices: 152 us -> none  [per_device(): lax.all_gather(cycle_integrals, 'tr', axis=3, tiled=True)]
    pallas_call x0 -> x1, Pallas kernels: none -> 83.9 us  [fused(): pl.pallas_call(kernel, out_shape=jax.ShapeDtypeStruct((64, 4096), BF16),...]
    reduce_scatter x1 -> x0, waiting for transfers between devices: 49.3 us -> none  [per_device(): lax.psum_scatter(moved_parts.astype(jnp.float32).astype(jnp.bfloat16), 'c...]
    unnamed x3 -> x1, local copies, waits for them, and re-layouts: 30.6 us -> 1.87 us
    all_to_all x2 -> x0, local copies, waits for them, and re-layouts: 24 us -> none  [per_device(): lax.all_to_all(partial_value.astype(jnp.bfloat16), 'tr', split_axis=3, co...]
    all_gather x1 -> x0, local copies, waits for them, and re-layouts: 21.3 us -> none  [per_device(): lax.all_gather(cycle_integrals, 'tr', axis=3, tiled=True)]
    convert_element_type x1 -> x0, local copies, waits for them, and re-layouts: 10 us -> none  [per_device(): partial_value.astype(jnp.bfloat16)]
  transfers between devices with their start and end apart: 2 -> 0, of which waited for: 2 -> 0; matrix products, arithmetic and copies ran while one was open for 1% -> 0% of each run, Pallas kernels for 0% -> 0%
where the time goes in v2:
time: 85.9 us; the launch traced here: 85.7 us
  Pallas kernels  83.9 us (98%)
  local copies, waits for them, and re-layouts  1.87 us (2%)
    pallas_call x1, Pallas kernels, fused(): pl.pallas_call(kernel, out_shape=jax.ShapeDtypeStruct((64, 4096), BF16),...  83.9 us
    unnamed x1, local copies, waits for them, and re-layouts  1.87 us

profile of v2, /device:TPU:1, one launch (start us, length us, event | category | flops | bytes accessed | tf_op | source)
XLA Modules:
  0.0 85.7 jit_solution(17752585078991329738)
XLA Ops:
  0.0 83.9 %cycle_fused.1 = bf16[64,4096]{1,0:T(8,128)(2,1)} custom-call(bf16[8,64,2,512]{3,2,1,0:T(2,128)(2,1)} %a_hbm.1, bf16[2,64,512]{2,1,0:T(8,128)(2,1)} %bitcast.5, s32[8,64]{1,0:T(8,128)} %live_hbm.1), custom_call_target="tpu_custom_call" | custom-call | tf_op jit(solution)/shard_map/cycle_fused/pallas_call | solution.py:297
  83.9 1.9 %copy.5 = bf16[1,64,1,4096]{3,1,2,0:T(8,128)(2,1)} copy(bf16[1,64,1,4096]{3,1,2,0:T(8,128)(2,1)} %bitcast.4) | data formatting | bytes 1048576

commit v3 on v2

--- a/solution.py
+++ b/solution.py
@@ -11,6 +11,8 @@
 F32 = jnp.float32
 BF16 = jnp.bfloat16
 NZ = 16
+GROUPS = ((0, 4), (4, 6), (6, 8))
+UNITS = [(stage, group) for stage in range(4) for group in range(3)]
 
 
 def dot_nt(lhs, rhs):
@@ -19,8 +21,8 @@
 
 def kernel(
     a_hbm, w_hbm, live_hbm, out_ref,
-    raw, live, aown, abuf, wbuf, kept, csend, crecv, y1send, y1recv, y2send, y2recv, psend, pieces,
-    s_in, s_a, s_af, r_a, s_w, r_w, s_c, r_c, s_y1, r_y1, s_y2, r_y2, s_p, r_p,
+    raw, live, aown, abuf, wbuf, kept, csend, crecv, y1send, y1recv, y2send, y2recv, psend, pieces, relay,
+    s_in, s_a, s_af, r_a, s_w, r_w, s_c, r_c, s_y1, r_y1, s_y2, r_y2, s_p, r_p, s_relay, r_relay,
 ):
     t_index = lax.axis_index("tr")
     c_index = lax.axis_index("ct")
@@ -109,82 +111,125 @@
         a_own(0, order).start()
         a_own(1, (order + 2) % 4).start()
 
-    def c_copy(t):
-        return rcopy(csend.at[t], crecv.at[t], s_c.at[t], r_c.at[t], mate)
-
-    def y1_copy(t, n):
-        return rcopy(y1send.at[t, n], y1recv.at[t, n], s_y1.at[t, n], r_y1.at[t, n],
-                     (ynear, yfar)[t % 2])
-
-    def y2_copy(t):
-        return rcopy(y2send.at[t], y2recv.at[t], s_y2.at[t], r_y2.at[t], (yfar, ynear)[t % 2])
-
-    def compute(t):
-        h = t % 2
-        blocks = aown if t < 2 else abuf.at[t // 2 - 1]
+    def rows_of(n):
+        lo, hi = GROUPS[UNITS[n][1]]
+        return pl.ds(lo * 64, (hi - lo) * 64)
+
+    def swapped(n):
+        stage, group = UNITS[n]
+        return (stage + (group > 0)) % 2
+
+    def c_copy(n):
+        part = (UNITS[n][0], slice(None), rows_of(n))
+        return rcopy(csend.at[part], crecv.at[part], s_c.at[n], r_c.at[n], mate)
+
+    def y1_copy(n, b):
+        part = (UNITS[n][0], b, rows_of(n))
+        return rcopy(y1send.at[part], y1recv.at[part], s_y1.at[n, b], r_y1.at[n, b],
+                     (ynear, yfar)[swapped(n)])
+
+    def y2_copy(n):
+        part = (UNITS[n][0], rows_of(n))
+        return rcopy(y2send.at[part], y2recv.at[part], s_y2.at[n], r_y2.at[n],
+                     (yfar, ynear)[swapped(n)])
+
+    def compute(n):
+        stage, group = UNITS[n]
+        lo, hi = GROUPS[group]
+        size = (hi - lo) * 64
+        blocks = abuf.at[stage - 1] if stage else aown
 
         def pair(p, carry):
-            total = jnp.zeros((512, 256), F32)
+            total = jnp.zeros((2 * size, 256), F32)
             for k in range(2):
-                mine = wbuf[q, h * 4:h * 4 + 4, k].reshape(256, 512)
-                theirs = wbuf[1 - q, h * 4:h * 4 + 4, k].reshape(256, 512)
+                mine = wbuf[q, lo:hi, k].reshape(size, 512)
+                theirs = wbuf[1 - q, lo:hi, k].reshape(size, 512)
                 rows = jnp.concatenate([mine, theirs], axis=0)
                 total = total + dot_nt(rows, blocks[k, pl.ds(pl.multiple_of(p * 256, 256), 256)])
-            for n in range(2):
-                cols = total[:, n * 128:(n + 1) * 128]
-                kept[t, p * 2 + n] = cols[:256]
-                csend[t, p * 2 + n] = cols[256:].astype(BF16)
+            for b in range(2):
+                cols = total[:, b * 128:(b + 1) * 128]
+                kept[stage, p * 2 + b, rows_of(n)] = cols[:size]
+                csend[stage, p * 2 + b, rows_of(n)] = cols[size:].astype(BF16)
             return carry
 
         lax.fori_loop(0, 2, pair, 0)
-        c_copy(t).start()
-
-    def core_sum(t):
-        near, far = (yn1, yn3) if t % 2 == 0 else (yn3, yn1)
-        c_copy(t).wait_recv()
-        y1send[t, 1] = (kept[t, yop] + crecv[t, yop].astype(F32)).astype(BF16)
-        y1_copy(t, 1).start()
-        y1send[t, 0] = (kept[t, near] + crecv[t, near].astype(F32)).astype(BF16)
-        y1_copy(t, 0).start()
-        kept[t, far] = kept[t, far] + crecv[t, far].astype(F32)
-        kept[t, y] = kept[t, y] + crecv[t, y].astype(F32)
-
-    def y_sum1(t):
-        far = (yn3, yn1)[t % 2]
-        y1_copy(t, 1).wait_recv()
-        y2send[t] = (kept[t, far] + y1recv[t, 1].astype(F32)).astype(BF16)
-        y2_copy(t).start()
+        c_copy(n).start()
+
+    def core_sum(n):
+        stage, rows = UNITS[n][0], rows_of(n)
+        near, far = (yn3, yn1) if swapped(n) else (yn1, yn3)
+        c_copy(n).wait_recv()
+        y1send[stage, 1, rows] = (kept[stage, yop, rows] + crecv[stage, yop, rows].astype(F32)).astype(BF16)
+        y1_copy(n, 1).start()
+        y1send[stage, 0, rows] = (kept[stage, near, rows] + crecv[stage, near, rows].astype(F32)).astype(BF16)
+        y1_copy(n, 0).start()
+        kept[stage, far, rows] = kept[stage, far, rows] + crecv[stage, far, rows].astype(F32)
+        kept[stage, y, rows] = kept[stage, y, rows] + crecv[stage, y, rows].astype(F32)
+
+    def y_sum1(n):
+        stage, rows = UNITS[n][0], rows_of(n)
+        far = yn1 if swapped(n) else yn3
+        y1_copy(n, 1).wait_recv()
+        y2send[stage, rows] = (kept[stage, far, rows] + y1recv[stage, 1, rows].astype(F32)).astype(BF16)
+        y2_copy(n).start()
 
     def off(slot):
         return (1 - q) * ((slot + 1) % 8) + q * (15 - slot)
 
-    def p_copy(t, s, i):
-        return rcopy(psend.at[t, s, i], pieces.at[t // 2, z], s_p.at[t, s, i], r_p.at[t // 2, z],
-                     dev(x, y, (z + off((t % 2) * 4 + s)) % NZ, i))
+    def p_copy(stage, slot, i):
+        return rcopy(psend.at[stage, slot, i], pieces.at[stage, z], s_p.at[stage, slot, i],
+                     r_p.at[stage, z], dev(x, y, (z + off(slot)) % NZ, i))
+
+    def half_way(stage, i):
+        return rcopy(psend.at[stage, 7, i], relay.at[stage, i], s_p.at[stage, 7, i],
+                     r_relay.at[stage, i], dev(x, y, (z + 12) % NZ, q))
+
+    def other_half(stage, i):
+        origin = (z + 4) % NZ
+        return rcopy(relay.at[stage, i], pieces.at[stage, origin], s_relay.at[stage, i],
+                     r_p.at[stage, origin], dev(x, y, (z + 12) % NZ, i))
+
+    def relay_on(stage):
+        @pl.when(q != 0)
+        def _():
+            for i in range(2):
+                half_way(stage, i).wait_recv()
+                other_half(stage, i).start()
 
     low = lax.broadcasted_iota(jnp.int32, (32, 128), 1) < 64
 
-    def y_sum2(t):
-        y1_copy(t, 0).wait_recv()
-        y2_copy(t).wait_recv()
-        for s in range(4):
-            rows = slice(s * 64, (s + 1) * 64)
-            full = kept[t, y, rows] + y1recv[t, 0, rows].astype(F32) + y2recv[t, rows].astype(F32)
+    def last_slot(stage, own, away):
+        @pl.when(q == 0)
+        def _():
+            own()
+
+        @pl.when(q != 0)
+        def _():
+            for i in range(2):
+                away(half_way(stage, i) if stage < 2 else p_copy(stage, 7, i))
+
+    def y_sum2(n):
+        stage, group = UNITS[n]
+        lo, hi = GROUPS[group]
+        y1_copy(n, 0).wait_recv()
+        y2_copy(n).wait_recv()
+        for slot in range(lo, hi):
+            rows = slice(slot * 64, (slot + 1) * 64)
+            full = (kept[stage, y, rows] + y1recv[stage, 0, rows].astype(F32)
+                    + y2recv[stage, rows].astype(F32))
             top, bottom = full[:32], full[32:]
-            psend[t, s, 0] = jnp.where(low, top, pltpu.roll(bottom, 64, 1)).astype(BF16)
-            psend[t, s, 1] = jnp.where(low, pltpu.roll(top, 64, 1), bottom).astype(BF16)
-        for s in range(4):
-            p_copy(t, s, 1).start()
-            if t % 2 == 1 and s == 3:
-                @pl.when(q == 0)
-                def _():
-                    pieces[t // 2, z] = psend[t, s, 0]
-
-                @pl.when(q != 0)
-                def _():
-                    p_copy(t, s, 0).start()
+            psend[stage, slot, 0] = jnp.where(low, top, pltpu.roll(bottom, 64, 1)).astype(BF16)
+            psend[stage, slot, 1] = jnp.where(low, pltpu.roll(top, 64, 1), bottom).astype(BF16)
+        for slot in range(hi - 1, lo - 1, -1):
+            if slot < 7:
+                p_copy(stage, slot, 0).start()
+                p_copy(stage, slot, 1).start()
             else:
-                p_copy(t, s, 0).start()
+                def own():
+                    pieces[stage, z] = psend[stage, 7, 0]
+                    p_copy(stage, 7, 1).start()
+
+                last_slot(stage, own, lambda copy: copy.start())
 
     def ring(step):
         for part in range(4):
@@ -201,54 +246,72 @@
 
     ring(2)
     ring(3)
-    forward(0)
     ring(4)
     ring(5)
     compute(0)
+    ring(6)
+    forward(0)
     forward(1)
-    ring(6)
     core_sum(0)
     ring(7)
     y_sum1(0)
+    compute(1)
     ring(8)
+    core_sum(1)
+    y_sum2(0)
+    a_own(1, 0).wait_recv()
+    a_own(1, 1).wait_recv()
+    a_own(0, 2).wait_recv()
+    a_own(0, 3).wait_recv()
+    compute(7)
     for part in range(2):
         w_hop(0, 8, part + 2).wait_recv()
         w_hop(1, 8, part).wait_recv()
-    compute(1)
-    a_own(0, 2).wait_recv()
-    a_own(0, 3).wait_recv()
+    compute(4)
+    compute(3)
+    y_sum1(1)
+    core_sum(7)
     compute(2)
-    core_sum(1)
-    y_sum2(0)
-    compute(3)
+    core_sum(4)
+    compute(5)
+    compute(8)
     core_sum(2)
-    a_own(1, 0).wait_recv()
-    a_own(1, 1).wait_recv()
-    compute(4)
-    core_sum(3)
-    compute(5)
-    core_sum(4)
-    y_sum1(1)
+    y_sum1(7)
     core_sum(5)
-    y_sum1(2)
-    y_sum1(3)
+    compute(6)
+    core_sum(8)
     y_sum2(1)
     y_sum1(4)
+    y_sum1(2)
+    core_sum(6)
+    y_sum2(7)
     for chunk in range(4):
         a_fwd(chunk // 2, chunk).wait_recv()
-    compute(6)
     y_sum1(5)
+    compute(11)
+    core_sum(3)
+    y_sum1(8)
     y_sum2(2)
-    compute(7)
-    core_sum(6)
-    y_sum2(3)
-    core_sum(7)
     y_sum2(4)
+    core_sum(11)
     y_sum2(5)
     y_sum1(6)
-    y_sum1(7)
+    compute(9)
+    y_sum1(3)
+    y_sum2(8)
+    compute(10)
+    y_sum1(11)
+    core_sum(9)
+    core_sum(10)
     y_sum2(6)
-    y_sum2(7)
+    y_sum2(3)
+    y_sum1(10)
+    y_sum1(9)
+    relay_on(1)
+    y_sum2(11)
+    relay_on(0)
+    y_sum2(10)
+    y_sum2(9)
 
     for stage in range(4):
         xs = (x + (0, 3, 1, 2)[stage]) % 4
@@ -277,19 +340,22 @@
             a_own(way, chunk).wait_send()
     for chunk in range(4):
         a_fwd(chunk // 2, chunk).wait_send()
-    for t in range(8):
-        c_copy(t).wait_send()
-        y1_copy(t, 0).wait_send()
-        y1_copy(t, 1).wait_send()
-        y2_copy(t).wait_send()
-        for s in range(4):
-            p_copy(t, s, 1).wait_send()
-            if t % 2 == 1 and s == 3:
-                @pl.when(q != 0)
-                def _():
-                    p_copy(t, s, 0).wait_send()
-            else:
-                p_copy(t, s, 0).wait_send()
+    for n in range(len(UNITS)):
+        c_copy(n).wait_send()
+        y1_copy(n, 0).wait_send()
+        y1_copy(n, 1).wait_send()
+        y2_copy(n).wait_send()
+    for stage in range(4):
+        for slot in range(7):
+            p_copy(stage, slot, 0).wait_send()
+            p_copy(stage, slot, 1).wait_send()
+        last_slot(stage, lambda: p_copy(stage, 7, 1).wait_send(), lambda copy: copy.wait_send())
+
+    @pl.when(q != 0)
+    def _():
+        for stage in range(2):
+            for i in range(2):
+                other_half(stage, i).wait_send()
 
 
 def fused(amplitudes, tiles, pair_live):
@@ -305,19 +371,20 @@
             pltpu.VMEM((2, 512, 512), BF16),
             pltpu.VMEM((3, 2, 512, 512), BF16),
             pltpu.VMEM((2, 8, 2, 64, 512), BF16),
-            pltpu.VMEM((8, 4, 256, 128), F32),
-            pltpu.VMEM((8, 4, 256, 128), BF16),
-            pltpu.VMEM((8, 4, 256, 128), BF16),
-            pltpu.VMEM((8, 2, 256, 128), BF16),
-            pltpu.VMEM((8, 2, 256, 128), BF16),
-            pltpu.VMEM((8, 256, 128), BF16),
-            pltpu.VMEM((8, 256, 128), BF16),
-            pltpu.VMEM((8, 4, 2, 32, 128), BF16),
+            pltpu.VMEM((4, 4, 512, 128), F32),
+            pltpu.VMEM((4, 4, 512, 128), BF16),
+            pltpu.VMEM((4, 4, 512, 128), BF16),
+            pltpu.VMEM((4, 2, 512, 128), BF16),
+            pltpu.VMEM((4, 2, 512, 128), BF16),
+            pltpu.VMEM((4, 512, 128), BF16),
+            pltpu.VMEM((4, 512, 128), BF16),
+            pltpu.VMEM((4, 8, 2, 32, 128), BF16),
             pltpu.VMEM((4, NZ, 32, 128), BF16),
+            pltpu.VMEM((2, 2, 32, 128), BF16),
             dma((6,)), dma((2, 4)), dma((4,)), dma((3, 4)),
             dma((2, 8, 4)), dma((2, 8, 4)),
-            dma((8,)), dma((8,)), dma((8, 2)), dma((8, 2)), dma((8,)), dma((8,)),
-            dma((8, 4, 2)), dma((4, NZ)),
+            dma((12,)), dma((12,)), dma((12, 2)), dma((12, 2)), dma((12,)), dma((12,)),
+            dma((4, 8, 2)), dma((4, NZ)), dma((2, 2)), dma((2, 2)),
         ],
         compiler_params=pltpu.CompilerParams(
             collective_id=0, has_side_effects=True, vmem_limit_bytes=56 * 1024 * 1024

time: 85.9 us -> 81.1 us (0.944)
  Pallas kernels: 83.9 us -> 79.1 us
    pallas_call x1, Pallas kernels: 83.9 us -> 79.1 us  [fused(): pl.pallas_call(kernel, out_shape=jax.ShapeDtypeStruct((64, 4096), BF16),...]
where the time goes in v3:
time: 81.1 us; the launch traced here: 81 us
  Pallas kernels  79.1 us (98%)
  local copies, waits for them, and re-layouts  1.87 us (2%)
    pallas_call x1, Pallas kernels, fused(): pl.pallas_call(kernel, out_shape=jax.ShapeDtypeStruct((64, 4096), BF16),...  79.1 us
    unnamed x1, local copies, waits for them, and re-layouts  1.87 us

profile of v3, /device:TPU:1, one launch (start us, length us, event | category | flops | bytes accessed | tf_op | source)
XLA Modules:
  0.0 81.0 jit_solution(9711625212593750641)
XLA Ops:
  0.0 79.1 %cycle_fused.1 = bf16[64,4096]{1,0:T(8,128)(2,1)} custom-call(bf16[8,64,2,512]{3,2,1,0:T(2,128)(2,1)} %a_hbm.1, bf16[2,64,512]{2,1,0:T(8,128)(2,1)} %bitcast.5, s32[8,64]{1,0:T(8,128)} %live_hbm.1), custom_call_target="tpu_custom_call" | custom-call | tf_op jit(solution)/shard_map/cycle_fused/pallas_call | solution.py:363
  79.1 1.9 %copy.5 = bf16[1,64,1,4096]{3,1,2,0:T(8,128)(2,1)} copy(bf16[1,64,1,4096]{3,1,2,0:T(8,128)(2,1)} %bitcast.4) | data formatting | bytes 1048576

commit v4 on v3

--- a/solution.py
+++ b/solution.py
@@ -387,7 +387,7 @@
             dma((4, 8, 2)), dma((4, NZ)), dma((2, 2)), dma((2, 2)),
         ],
         compiler_params=pltpu.CompilerParams(
-            collective_id=0, has_side_effects=True, vmem_limit_bytes=56 * 1024 * 1024
+            collective_id=0, has_side_effects=True, vmem_limit_bytes=40 * 1024 * 1024
         ),
         name="cycle_fused",
     )(amplitudes, tiles, pair_live)
@@ -395,7 +395,11 @@
 
 def per_device(amplitudes, cycle_integrals, pair_live):
     tiles = cycle_integrals[:, :, 0, :].transpose(0, 2, 1)
-    return fused(amplitudes, tiles, pair_live).reshape(1, 64, 1, 4096)
+    operands = [
+        pltpu.with_memory_space_constraint(operand, pltpu.HBM)
+        for operand in (amplitudes, tiles, pair_live)
+    ]
+    return fused(*operands).reshape(1, 64, 1, 4096)
 
 
 def solution(mesh):

time: 81.1 us -> 79.2 us (0.977)
  local copies, waits for them, and re-layouts: 1.87 us -> 0.8 us
    unnamed x1, local copies, waits for them, and re-layouts: 1.87 us -> 0.8 us
where the time goes in v4:
time: 79.2 us; the launch traced here: 79.1 us
  Pallas kernels  78.3 us (99%)
  local copies, waits for them, and re-layouts  0.8 us (1%)
    pallas_call x1, Pallas kernels, fused(): pl.pallas_call(kernel, out_shape=jax.ShapeDtypeStruct((64, 4096), BF16),...  78.3 us

profile of v4, /device:TPU:1, one launch (start us, length us, event | category | flops | bytes accessed | tf_op | source)
XLA Modules:
  0.0 79.1 jit_solution(13656179975325380041)
XLA Ops:
  0.0 78.3 %cycle_fused.1 = bf16[64,4096]{1,0:T(8,128)(2,1)S(1)} custom-call(bf16[8,64,2,512]{3,2,1,0:T(2,128)(2,1)} %a_hbm.1, bf16[2,64,512]{2,1,0:T(8,128)(2,1)} %bitcast.5, s32[8,64]{1,0:T(8,128)} %live_hbm.1), custom_call_target="tpu_custom_call" | custom-call | tf_op jit(solution)/shard_map/cycle_fused/pallas_call | solution.py:363
  78.3 0.8 %copy.5 = bf16[1,64,1,4096]{3,1,2,0:T(8,128)(2,1)} copy(bf16[1,64,1,4096]{3,1,2,0:T(8,128)(2,1)S(1)} %bitcast.4) | data formatting | bytes 1048576

commit v5 on v4

--- a/solution.py
+++ b/solution.py
@@ -139,20 +139,17 @@
         size = (hi - lo) * 64
         blocks = abuf.at[stage - 1] if stage else aown
 
-        def pair(p, carry):
-            total = jnp.zeros((2 * size, 256), F32)
-            for k in range(2):
-                mine = wbuf[q, lo:hi, k].reshape(size, 512)
-                theirs = wbuf[1 - q, lo:hi, k].reshape(size, 512)
-                rows = jnp.concatenate([mine, theirs], axis=0)
-                total = total + dot_nt(rows, blocks[k, pl.ds(pl.multiple_of(p * 256, 256), 256)])
+        rows = jnp.concatenate([
+            jnp.concatenate([wbuf[core, lo:hi, k].reshape(size, 512) for k in range(2)], axis=1)
+            for core in (q, 1 - q)
+        ], axis=0)
+        for p in range(2):
+            cols = slice(p * 256, p * 256 + 256)
+            total = dot_nt(rows, jnp.concatenate([blocks[0, cols], blocks[1, cols]], axis=1))
             for b in range(2):
-                cols = total[:, b * 128:(b + 1) * 128]
-                kept[stage, p * 2 + b, rows_of(n)] = cols[:size]
-                csend[stage, p * 2 + b, rows_of(n)] = cols[size:].astype(BF16)
-            return carry
-
-        lax.fori_loop(0, 2, pair, 0)
+                half = total[:, b * 128:(b + 1) * 128]
+                kept[stage, p * 2 + b, rows_of(n)] = half[:size]
+                csend[stage, p * 2 + b, rows_of(n)] = half[size:].astype(BF16)
         c_copy(n).start()
 
     def core_sum(n):

time: 79.2 us -> 78.3 us (0.989)
  Pallas kernels: 78.3 us -> 77.3 us
    pallas_call x1, Pallas kernels: 78.3 us -> 77.3 us  [fused(): pl.pallas_call(kernel, out_shape=jax.ShapeDtypeStruct((64, 4096), BF16),...]
where the time goes in v5:
time: 78.3 us; the launch traced here: 78.2 us
  Pallas kernels  77.3 us (99%)
  local copies, waits for them, and re-layouts  0.8 us (1%)
    pallas_call x1, Pallas kernels, fused(): pl.pallas_call(kernel, out_shape=jax.ShapeDtypeStruct((64, 4096), BF16),...  77.3 us

profile of v5, /device:TPU:1, one launch (start us, length us, event | category | flops | bytes accessed | tf_op | source)
XLA Modules:
  0.0 78.2 jit_solution(14813091107569269623)
XLA Ops:
  0.0 77.3 %cycle_fused.1 = bf16[64,4096]{1,0:T(8,128)(2,1)S(1)} custom-call(bf16[8,64,2,512]{3,2,1,0:T(2,128)(2,1)} %a_hbm.1, bf16[2,64,512]{2,1,0:T(8,128)(2,1)} %bitcast.5, s32[8,64]{1,0:T(8,128)} %live_hbm.1), custom_call_target="tpu_custom_call" | custom-call | tf_op jit(solution)/shard_map/cycle_fused/pallas_call | solution.py:360
  77.4 0.8 %copy.5 = bf16[1,64,1,4096]{3,1,2,0:T(8,128)(2,1)} copy(bf16[1,64,1,4096]{3,1,2,0:T(8,128)(2,1)S(1)} %bitcast.4) | data formatting | bytes 1048576

commit v6 on v5

--- a/solution.py
+++ b/solution.py
@@ -310,24 +310,6 @@
     y_sum2(10)
     y_sum2(9)
 
-    for stage in range(4):
-        xs = (x + (0, 3, 1, 2)[stage]) % 4
-
-        def arrive(n, carry):
-            @pl.when((n != z) | (q != 0))
-            def _():
-                rcopy(psend.at[0, 0, 0], pieces.at[stage, n], s_p.at[0, 0, 0], r_p.at[stage, n],
-                      mate).wait_recv()
-
-            return carry
-
-        lax.fori_loop(0, NZ, arrive, 0)
-        for m in range(NZ // 2):
-            even, odd = pieces[stage, 2 * m].astype(F32), pieces[stage, 2 * m + 1].astype(F32)
-            cols = pl.ds(pl.multiple_of(xs * 1024 + m * 128, 128), 128)
-            out_ref[0:32, cols] = jnp.where(low, even, pltpu.roll(odd, 64, 1)).astype(BF16)
-            out_ref[32:64, cols] = jnp.where(low, pltpu.roll(even, 64, 1), odd).astype(BF16)
-
     for way in range(2):
         for n in range(1, 9):
             for part in range(4):
@@ -342,6 +324,28 @@
         y1_copy(n, 0).wait_send()
         y1_copy(n, 1).wait_send()
         y2_copy(n).wait_send()
+
+    def unpack(stage):
+        xs = (x + (0, 3, 1, 2)[stage]) % 4
+
+        def arrive(n, carry):
+            @pl.when((n != z) | (q != 0))
+            def _():
+                rcopy(psend.at[0, 0, 0], pieces.at[stage, n], s_p.at[0, 0, 0], r_p.at[stage, n],
+                      mate).wait_recv()
+
+            return carry
+
+        lax.fori_loop(0, NZ, arrive, 0)
+        for m in range(NZ // 2):
+            even, odd = pieces[stage, 2 * m].astype(F32), pieces[stage, 2 * m + 1].astype(F32)
+            cols = pl.ds(pl.multiple_of(xs * 1024 + m * 128, 128), 128)
+            out_ref[0:32, cols] = jnp.where(low, even, pltpu.roll(odd, 64, 1)).astype(BF16)
+            out_ref[32:64, cols] = jnp.where(low, pltpu.roll(even, 64, 1), odd).astype(BF16)
+
+    for stage in range(3):
+        unpack(stage)
+
     for stage in range(4):
         for slot in range(7):
             p_copy(stage, slot, 0).wait_send()
@@ -353,6 +357,8 @@
         for stage in range(2):
             for i in range(2):
                 other_half(stage, i).wait_send()
+
+    unpack(3)
 
 
 def fused(amplitudes, tiles, pair_live):

time: 78.3 us -> 78 us (level)
  no operation moved by 1% of the time
where the time goes in v6:
time: 78 us; the launch traced here: 77.9 us
  Pallas kernels  77.1 us (99%)
  local copies, waits for them, and re-layouts  0.8 us (1%)
    pallas_call x1, Pallas kernels, fused(): pl.pallas_call(kernel, out_shape=jax.ShapeDtypeStruct((64, 4096), BF16),...  77.1 us

profile of v6, /device:TPU:1, one launch (start us, length us, event | category | flops | bytes accessed | tf_op | source)
XLA Modules:
  0.0 77.9 jit_solution(12405988715726303782)
XLA Ops:
  0.0 77.1 %cycle_fused.1 = bf16[64,4096]{1,0:T(8,128)(2,1)S(1)} custom-call(bf16[8,64,2,512]{3,2,1,0:T(2,128)(2,1)} %a_hbm.1, bf16[2,64,512]{2,1,0:T(8,128)(2,1)} %bitcast.5, s32[8,64]{1,0:T(8,128)} %live_hbm.1), custom_call_target="tpu_custom_call" | custom-call | tf_op jit(solution)/shard_map/cycle_fused/pallas_call | solution.py:366
  77.1 0.8 %copy.5 = bf16[1,64,1,4096]{3,1,2,0:T(8,128)(2,1)} copy(bf16[1,64,1,4096]{3,1,2,0:T(8,128)(2,1)S(1)} %bitcast.4) | data formatting | bytes 1048576

commit v7 on v6

--- a/solution.py
+++ b/solution.py
@@ -96,8 +96,8 @@
             for k in range(2):
                 aown[k, i * 64:(i + 1) * 64] = both[k] * (col[k] * row).astype(BF16)
 
-    mask_chunk(0)
-    mask_chunk(2)
+    for chunk in (0, 2, 1, 3):
+        mask_chunk(chunk)
     w_in.wait()
     pl.semaphore_wait(barrier, 7)
     for part in range(4):
@@ -105,8 +105,6 @@
             w_hop(way, 1, part).start()
     a_own(0, 0).start()
     a_own(1, 2).start()
-    mask_chunk(1)
-    mask_chunk(3)
     for order in range(1, 4):
         a_own(0, order).start()
         a_own(1, (order + 2) % 4).start()

time: 78 us -> 78 us (level)
  no operation moved by 1% of the time
where the time goes in v7:
time: 78 us; the launch traced here: 77.9 us
  Pallas kernels  77.1 us (99%)
  local copies, waits for them, and re-layouts  0.8 us (1%)
    pallas_call x1, Pallas kernels, fused(): pl.pallas_call(kernel, out_shape=jax.ShapeDtypeStruct((64, 4096), BF16),...  77.1 us

profile of v7, /device:TPU:1, one launch (start us, length us, event | category | flops | bytes accessed | tf_op | source)
XLA Modules:
  0.0 77.9 jit_solution(17828744649651701798)
XLA Ops:
  0.0 77.1 %cycle_fused.1 = bf16[64,4096]{1,0:T(8,128)(2,1)S(1)} custom-call(bf16[8,64,2,512]{3,2,1,0:T(2,128)(2,1)} %a_hbm.1, bf16[2,64,512]{2,1,0:T(8,128)(2,1)} %bitcast.5, s32[8,64]{1,0:T(8,128)} %live_hbm.1), custom_call_target="tpu_custom_call" | custom-call | tf_op jit(solution)/shard_map/cycle_fused/pallas_call | solution.py:364
  77.1 0.8 %copy.5 = bf16[1,64,1,4096]{3,1,2,0:T(8,128)(2,1)} copy(bf16[1,64,1,4096]{3,1,2,0:T(8,128)(2,1)S(1)} %bitcast.4) | data formatting | bytes 1048576
